TPU v7x, 32 devices: a whole 2x2x4 slice. The times are simulated.
32 devices in a mesh: row: 4 (over y, x), col: 8 (over z, core).
Axes of the slice: x: 2, y: 2, z: 4, core: 2. Of those that a mesh axis runs over, the one named last changes fastest.
Arguments:
- amplitudes: bfloat16 [4096, 16384], P('col', 'row'), may hold values from -6 to 6
- integrals: bfloat16 [4096, 16384], P('row', 'col'), may hold values from -0.09375 to 0.09375
- tile_mask: int32 [64, 256], P(None, 'row'), may hold values from 0 to 1, as said below
- occ_energy: float32 [4], replicated, may hold values from -1 to -0.2
- virt_energy: float32 [4096], replicated, may hold values from 0.2 to 1.5
Outputs:
- update: bfloat16 [16384, 16384], P(('row', 'col'))
Inputs may be any that keep to these rules, and one draw needn't show every extreme that they name: `tile_mask`: 0 drops a tile, 1 keeps it; the share of kept tiles differs strongly between groups of (ia) rows.
All inputs are finite; a program needn't handle non-finite values.
Results may differ from a plain program's by a relative error of at most 0.0049.
Values may be sent and summed in bfloat16 or wider, within the bound.
A program may use at most 192 MiB of HBM per device.

v0:
```python
import jax
import jax.numpy as jnp
from jax import lax
from jax.sharding import PartitionSpec as P

TILE = 64


def local(amplitudes, integrals, tile_mask, occ_energy, virt_energy):
    col_count = lax.axis_size("col")
    row_place = lax.axis_index("row")
    col_place = lax.axis_index("col")
    local_depth, local_width = amplitudes.shape
    tile_rows = local_depth // TILE
    tile_cols = local_width // TILE
    own_mask = lax.dynamic_slice_in_dim(tile_mask, col_place * tile_rows, tile_rows, 0)
    keep_tiles = own_mask.astype(jnp.bfloat16)
    masked = (
        amplitudes.reshape(tile_rows, TILE, tile_cols, TILE) * keep_tiles[:, None, :, None]
    ).reshape(local_depth, local_width)
    whole_panel = lax.all_gather(integrals, "row", axis=0, tiled=True)
    left_rows = lax.all_gather(masked, "col", axis=0, tiled=True)
    product_block = lax.dot_general(
        left_rows, whole_panel, (((0,), (0,)), ((), ())), preferred_element_type=jnp.float32
    )
    cycle_block = product_block.astype(jnp.bfloat16)
    flat_rows = lax.all_to_all(cycle_block, "col", split_axis=0, concat_axis=1, tiled=True)
    rows_here, total_cols = flat_rows.shape
    pieces = total_cols // rows_here
    arrived = lax.all_to_all(
        flat_rows.reshape(rows_here, pieces, rows_here),
        ("row", "col"),
        split_axis=1,
        concat_axis=1,
        tiled=True,
    )
    mirrored = jnp.transpose(arrived, (2, 1, 0)).reshape(rows_here, total_cols)
    pair_gap = (virt_energy[None, :] - occ_energy[:, None]).reshape(total_cols)
    flat_place = row_place * col_count + col_place
    row_gap = lax.dynamic_slice_in_dim(pair_gap, flat_place * rows_here, rows_here, 0)
    summed = flat_rows.astype(jnp.float32) + mirrored.astype(jnp.float32)
    return (summed / (row_gap[:, None] + pair_gap[None, :])).astype(jnp.bfloat16)


def solution(mesh):
    return jax.shard_map(
        local,
        mesh=mesh,
        in_specs=(P("col", "row"), P("row", "col"), P(None, "row"), P(), P()),
        out_specs=P(("row", "col"), None),
        check_vma=False,
    )
```

profile of v0, /device:TPU:0, one launch (start us, length us, event | category | flops | bytes accessed | tf_op | source)
XLA Modules:
  0.0 1402.9 jit_solution(14816292952681816901)
XLA Ops:
  6.5 0.0 all-gather.5.cloned.1.call-start
  6.5 0.7 all-gather.5.cloned.1.call-update
  7.3 0.0 all-gather.3.cloned.1.call-start
  7.3 0.7 dynamic-slice_convert_fusion
  8.0 5.6 mul.21
  13.6 12.6 mul.22
  26.3 7.9 mul.23
  34.1 0.0 all-gather.3.cloned.1.call-update
  34.2 135.1 %all-gather.5.cloned.1.call-done = bf16[4096,2048]{1,0:T(8,128)(2,1)} async-done(((bf16[1024,2048]{1,0:T(8,128)(2,1)}), bf16[4096,2048]{1,0:T(8,128)(2,1)}) %all-gather.5.cloned.1.call-update) | async-done | bytes 16777232 | tf_op jit(solution)/shard_map/all_gather | solution.py:21
  169.2 290.2 %all-gather.3.cloned.1.call-done = bf16[4096,4096]{1,0:T(8,128)(2,1)} async-done(((bf16[512,4096]{1,0:T(8,128)(2,1)}), bf16[4096,4096]{1,0:T(8,128)(2,1)}) %all-gather.3.cloned.1.call-update) | async-done | bytes 33554448 | tf_op jit(solution)/shard_map/all_gather | solution.py:22
  459.4 79.4 %convolution_convert_fusion = bf16[4096,2048]{1,0:T(8,128)(2,1)} fusion(bf16[4096,4096]{1,0:T(8,128)(2,1)} %all-gather.3.cloned.1.call-done, bf16[4096,2048]{1,0:T(8,128)(2,1)} %all-gather.5.cloned.1.call-done), kind=kOutput, calls=%fused_computation.4 | convolution fusion | flops 68727865344 | bytes 67108864 | tf_op jit(solution)/shard_map/dot_general | solution.py:23
  538.9 21.6 %copy.9 = bf16[8,512,2048]{1,2,0:T(8,128)(2,1)} copy(bf16[8,512,2048]{2,1,0:T(8,128)(2,1)} %bitcast.20) | data formatting | bytes 33554432 | tf_op jit(solution)/shard_map/all_to_all | solution.py:27
  560.5 371.1 %all_to_all.21 = bf16[8,512,2048]{1,2,0:T(8,128)(2,1)} all-to-all(bf16[8,512,2048]{1,2,0:T(8,128)(2,1)} %copy.9), channel_id=1, replica_groups=mesh['row'=4,'col'=8] {'col'}, dimensions={0} | all-to-all | bytes 33554432 | tf_op jit(solution)/shard_map/all_to_all | solution.py:27
  931.6 0.0 copy-start.1
  931.6 4.0 all-to-all-start.1
  935.7 0.0 copy-done
  935.7 0.0 copy-done.1
  935.7 0.1 subtract_bitcast_fusion
  935.8 0.1 dynamic_slice.7
  935.9 364.4 %all-to-all-done.1 = bf16[512,32,512]{0,2,1:T(8,128)(2,1)} async-done(((bf16[512,32,512]{0,2,1:T(8,128)(2,1)}), bf16[512,32,512]{0,2,1:T(8,128)(2,1)}, u32[]{:S(2)}, u32[]{:S(2)}) %all-to-all-start.1) | async-done | bytes 16777248 | tf_op jit(solution)/shard_map/all_to_all | solution.py:30
  1300.2 18.8 %convert_bitcast_fusion = f32[512,32,512]{2,0,1:T(8,128)} fusion(bf16[512,32,512]{0,2,1:T(8,128)(2,1)} %all-to-all-done.1), kind=kLoop, calls=%fused_computation.3 | loop fusion | flops 8388608 | bytes 50331648 | tf_op jit(solution)/shard_map/convert_element_type | solution.py:41
  1319.0 33.4 %copy.10 = f32[512,32,512]{0,2,1:T(8,128)} copy(f32[512,32,512]{2,0,1:T(8,128)} %convert_bitcast_fusion) | data formatting | bytes 67108864 | tf_op jit(solution)/shard_map/convert_element_type | solution.py:41
  1352.4 22.5 %fusion.1 = bf16[512,16384]{0,1:T(8,128)(2,1)} fusion(f32[512,32,512]{0,2,1:T(8,128)} %copy.10, bf16[8,512,2048]{1,2,0:T(8,128)(2,1)} %all_to_all.21, f32[16384]{0:T(1024)S(1)} %bitcast.22, f32[512]{0:T(512)S(1)} %dynamic_slice.7), kind=kLoop, calls=%fused_computation.2 | loop fusion | flops 41943040 | bytes 67176448 | tf_op jit(solution)/shard_map/convert_element_type | solution.py:42
  1374.9 21.2 %copy.11 = bf16[512,16384]{1,0:T(8,128)(2,1)} copy(bf16[512,16384]{0,1:T(8,128)(2,1)} %fusion.1) | data formatting | bytes 33554432 | tf_op jit(solution)/shard_map/convert_element_type | solution.py:42
  (2 shorter events, 0.0 us)
Async XLA Ops:
  6.5 162.7 %all-gather.5.cloned.1.call-start = ((), (), s32[]{:S(2)}) async-start(), calls=%async_computation.3 | async-start | bytes 20971520 | tf_op jit(solution)/shard_map/all_gather | solution.py:21
  7.3 452.2 %all-gather.3.cloned.1.call-start = ((), (), s32[]{:S(2)}) async-start(), calls=%async_computation.2 | async-start | bytes 37748736 | tf_op jit(solution)/shard_map/all_gather | solution.py:22
  931.6 4.0 copy-start
  931.6 4.0 copy-start.1
  931.6 368.6 %all-to-all-start.1 = ((bf16[512,32,512]{0,2,1:T(8,128)(2,1)}), bf16[512,32,512]{0,2,1:T(8,128)(2,1)}, u32[]{:S(2)}, u32[]{:S(2)}) async-start(bf16[512,32,512]{0,2,1:T(8,128)(2,1)} %bitcast.19), calls=%async_computation.1 | async-start | bytes 33554432 | tf_op jit(solution)/shard_map/all_to_all | solution.py:30
Sparse Core Ops, SparseCore 0:
  9.2 160.0 all-gather.4
  170.8 288.5 all-gather.2
where the time goes:
time: 1410 us; the launch traced here: 1400 us
  waiting for transfers between devices  790 us (56%)
  blocking collectives  371 us (26%)
  local copies, waits for them, and re-layouts  94.5 us (7%)
  matrix products  79.4 us (6%)
  other arithmetic  50 us (4%)
    all_to_all x1, blocking collectives, local(): lax.all_to_all(cycle_block, 'col', split_axis=0, concat_axis=1, tiled=True)  371 us
    all_to_all x1, waiting for transfers between devices, local(): lax.all_to_all(flat_rows.reshape(rows_here, pieces, rows_here), ('row', '...  364 us
    all_gather x1, waiting for transfers between devices, local(): left_rows = lax.all_gather(masked, 'col', axis=0, tiled=True)  290 us
    all_gather x1, waiting for transfers between devices, local(): whole_panel = lax.all_gather(integrals, 'row', axis=0, tiled=True)  135 us
    dot_general x1, matrix products, local(): lax.dot_general(left_rows, whole_panel, (((0,), (0,)), ((), ())), preferr...  79.4 us
    convert_element_type x1, local copies, waits for them, and re-layouts, local(): summed = flat_rows.astype(jnp.float32) + mirrored.astype(jnp.float32)  33.4 us
  transfers between devices with their start and end apart: 3, of which 3 were waited for; matrix products, arithmetic and copies ran while one was open for 2% of the time, Pallas kernels for 0%

commit v1 on v0

--- a/solution.py
+++ b/solution.py
@@ -18,7 +18,22 @@
     masked = (
         amplitudes.reshape(tile_rows, TILE, tile_cols, TILE) * keep_tiles[:, None, :, None]
     ).reshape(local_depth, local_width)
-    whole_panel = lax.all_gather(integrals, "row", axis=0, tiled=True)
+    ways, here, step = (lax.axis_size("row"), lax.axis_index("row"), integrals.shape[0])
+    shape = [n * ways if d == 0 else n for d, n in enumerate(integrals.shape)]
+    whole_panel = lax.dynamic_update_slice_in_dim(
+        jnp.zeros(shape, integrals.dtype), integrals, here * step, axis=0
+    )
+    going_up = going_down = integrals
+    for far in range(1, ways // 2 + 1):
+        going_up = lax.ppermute(going_up, "row", [(d, (d + 1) % ways) for d in range(ways)])
+        whole_panel = lax.dynamic_update_slice_in_dim(
+            whole_panel, going_up, (here - far) % ways * step, axis=0
+        )
+        if 2 * far < ways:
+            going_down = lax.ppermute(going_down, "row", [(d, (d - 1) % ways) for d in range(ways)])
+            whole_panel = lax.dynamic_update_slice_in_dim(
+                whole_panel, going_down, (here + far) % ways * step, axis=0
+            )
     left_rows = lax.all_gather(masked, "col", axis=0, tiled=True)
     product_block = lax.dot_general(
         left_rows, whole_panel, (((0,), (0,)), ((), ())), preferred_element_type=jnp.float32

time: 1410 us -> 1270 us (0.901)
  waiting for transfers between devices: 790 us -> 627 us
  local copies, waits for them, and re-layouts: 94.5 us -> 118 us
    all_gather x1, waiting for transfers between devices: 290 us -> 12.1 us  [local(): left_rows = lax.all_gather(masked, 'col', axis=0, tiled=True)]
    ppermute x0 -> x3, waiting for transfers between devices: none -> 251 us  [the longest x2 175 us: local(): lax.ppermute(going_up, 'row', [(d, (d + 1) % ways) for d in range(ways)])]
    all_gather x1 -> x0, waiting for transfers between devices: 135 us -> none  [local(): whole_panel = lax.all_gather(integrals, 'row', axis=0, tiled=True)]
    dynamic_update_slice x0 -> x4, local copies, waits for them, and re-layouts: none -> 16.9 us  [the longest x2 9.57 us: local(): lax.dynamic_update_slice_in_dim(whole_panel, going_up, (here - far) % way...]
  transfers between devices with their start and end apart: 3 -> 5, of which waited for: 3 -> 5; matrix products, arithmetic and copies ran while one was open for 2% -> 2% of each run, Pallas kernels for 0% -> 0%
where the time goes in v1:
time: 1270 us
  waiting for transfers between devices  627 us (49%)
  blocking collectives  371 us (29%)
  local copies, waits for them, and re-layouts  118 us (9%)
  matrix products  79.5 us (6%)
  other arithmetic  49.3 us (4%)
  between operations  13.4 us (1%)
    all_to_all x1, blocking collectives, local(): lax.all_to_all(cycle_block, 'col', split_axis=0, concat_axis=1, tiled=True)  371 us
    all_to_all x1, waiting for transfers between devices, local(): lax.all_to_all(flat_rows.reshape(rows_here, pieces, rows_here), ('row', '...  364 us
    ppermute x2, waiting for transfers between devices, local(): lax.ppermute(going_up, 'row', [(d, (d + 1) % ways) for d in range(ways)])  175 us
    dot_general x1, matrix products, local(): lax.dot_general(left_rows, whole_panel, (((0,), (0,)), ((), ())), preferr...  79.5 us
    ppermute x1, waiting for transfers between devices, local(): lax.ppermute(going_down, 'row', [(d, (d - 1) % ways) for d in range(ways)])  75.4 us
    convert_element_type x1, local copies, waits for them, and re-layouts, local(): summed = flat_rows.astype(jnp.float32) + mirrored.astype(jnp.float32)  33.4 us
  transfers between devices with their start and end apart: 5, of which 5 were waited for; matrix products, arithmetic and copies ran while one was open for 2% of the time, Pallas kernels for 0%

profile of v1, /device:TPU:0, one launch (start us, length us, event | category | flops | bytes accessed | tf_op | source)
XLA Modules:
  0.0 1267.1 jit_solution(10143293611574722081)
XLA Ops:
  7.2 5.6 mul.33
  12.8 12.0 mul.34
  24.9 7.2 mul.35
  32.1 3.0 collective-permute-start
  35.1 1.0 collective-permute-start.1
  36.1 91.7 %collective-permute-done = bf16[1024,2048]{1,0:T(8,128)(2,1)} collective-permute-done((bf16[1024,2048]{1,0:T(8,128)(2,1)}, bf16[1024,2048]{1,0:T(8,128)(2,1)}, u32[]{:S(2)}, u32[]{:S(2)}) %collective-permute-start) | collective-permute-done | bytes 4194336 | tf_op jit(solution)/shard_map/ppermute | solution.py:28
  127.8 1.1 collective-permute-start.2
  128.8 6.8 broadcast_in_dim.2
  135.7 2.3 constant_dynamic-update-slice_fusion.3
  138.0 4.8 constant_dynamic-update-slice_fusion.2
  142.8 75.4 %collective-permute-done.1 = bf16[1024,2048]{1,0:T(8,128)(2,1)} collective-permute-done((bf16[1024,2048]{1,0:T(8,128)(2,1)}, bf16[1024,2048]{1,0:T(8,128)(2,1)}, u32[]{:S(2)}, u32[]{:S(2)}) %collective-permute-start.1) | collective-permute-done | bytes 4194336 | tf_op jit(solution)/shard_map/ppermute | solution.py:33
  218.2 5.0 constant_dynamic-update-slice_fusion.1
  223.2 83.5 %collective-permute-done.2 = bf16[1024,2048]{1,0:T(8,128)(2,1)} collective-permute-done((bf16[1024,2048]{1,0:T(8,128)(2,1)}, bf16[1024,2048]{1,0:T(8,128)(2,1)}, u32[]{:S(2)}, u32[]{:S(2)}) %collective-permute-start.2) | collective-permute-done | bytes 4194336 | tf_op jit(solution)/shard_map/ppermute | solution.py:28
  306.7 4.8 constant_dynamic-update-slice_fusion
  311.5 12.1 all-gather.2.cloned.1.call-done
  323.5 79.5 %convolution_convert_fusion = bf16[4096,2048]{1,0:T(8,128)(2,1)} fusion(bf16[4096,4096]{1,0:T(8,128)(2,1)} %all-gather.2.cloned.1.call-done, bf16[4096,2048]{1,0:T(8,128)(2,1)} %constant_dynamic-update-slice_fusion), kind=kOutput, calls=%fused_computation.4 | convolution fusion | flops 68727865344 | bytes 67108864 | tf_op jit(solution)/shard_map/dot_general | solution.py:38
  403.1 21.5 %copy.9 = bf16[8,512,2048]{1,2,0:T(8,128)(2,1)} copy(bf16[8,512,2048]{2,1,0:T(8,128)(2,1)} %bitcast.20) | data formatting | bytes 33554432 | tf_op jit(solution)/shard_map/all_to_all | solution.py:42
  424.6 371.2 %all_to_all.21 = bf16[8,512,2048]{1,2,0:T(8,128)(2,1)} all-to-all(bf16[8,512,2048]{1,2,0:T(8,128)(2,1)} %copy.9), channel_id=1, replica_groups=mesh['row'=4,'col'=8] {'col'}, dimensions={0} | all-to-all | bytes 33554432 | tf_op jit(solution)/shard_map/all_to_all | solution.py:42
  795.8 4.0 all-to-all-start.1
  800.0 364.3 %all-to-all-done.1 = bf16[512,32,512]{0,2,1:T(8,128)(2,1)} async-done(((bf16[512,32,512]{0,2,1:T(8,128)(2,1)}), bf16[512,32,512]{0,2,1:T(8,128)(2,1)}, u32[]{:S(2)}, u32[]{:S(2)}) %all-to-all-start.1) | async-done | bytes 16777248 | tf_op jit(solution)/shard_map/all_to_all | solution.py:45
  1164.3 18.8 %convert_bitcast_fusion = f32[512,32,512]{2,0,1:T(8,128)} fusion(bf16[512,32,512]{0,2,1:T(8,128)(2,1)} %all-to-all-done.1), kind=kLoop, calls=%fused_computation.3 | loop fusion | flops 8388608 | bytes 50331648 | tf_op jit(solution)/shard_map/convert_element_type | solution.py:56
  1183.2 33.4 %copy.10 = f32[512,32,512]{0,2,1:T(8,128)} copy(f32[512,32,512]{2,0,1:T(8,128)} %convert_bitcast_fusion) | data formatting | bytes 67108864 | tf_op jit(solution)/shard_map/convert_element_type | solution.py:56
  1216.5 22.5 %fusion.1 = bf16[512,16384]{0,1:T(8,128)(2,1)} fusion(f32[512,32,512]{0,2,1:T(8,128)} %copy.10, bf16[8,512,2048]{1,2,0:T(8,128)(2,1)} %all_to_all.21, f32[16384]{0:T(1024)S(1)} %bitcast.22, f32[512]{0:T(512)S(1)} %dynamic_slice.7), kind=kLoop, calls=%fused_computation.2 | loop fusion | flops 41943040 | bytes 67176448 | tf_op jit(solution)/shard_map/convert_element_type | solution.py:57
  1239.1 21.2 %copy.11 = bf16[512,16384]{1,0:T(8,128)(2,1)} copy(bf16[512,16384]{0,1:T(8,128)(2,1)} %fusion.1) | data formatting | bytes 33554432 | tf_op jit(solution)/shard_map/convert_element_type | solution.py:57
  (12 shorter events, 0.9 us)
Async XLA Ops:
  6.5 317.0 %all-gather.2.cloned.1.call-start = ((), (), s32[]{:S(2)}) async-start(), calls=%async_computation.2 | async-start | bytes 37748736 | tf_op jit(solution)/shard_map/all_gather | solution.py:37
  32.1 95.7 %collective-permute-start = (bf16[1024,2048]{1,0:T(8,128)(2,1)}, bf16[1024,2048]{1,0:T(8,128)(2,1)}, u32[]{:S(2)}, u32[]{:S(2)}) collective-permute-start(bf16[1024,2048]{1,0:T(8,128)(2,1)} %param.6), channel_id=1, source_target_pairs={{0,8},{8,16},{16,24},{24,0},{1,9},{9,17},{17,25},{25,1},{2,10},{10... | collective-permute-start | bytes 12582920 | tf_op jit(solution)/shard_map/ppermute | solution.py:28
  35.1 183.1 %collective-permute-start.1 = (bf16[1024,2048]{1,0:T(8,128)(2,1)}, bf16[1024,2048]{1,0:T(8,128)(2,1)}, u32[]{:S(2)}, u32[]{:S(2)}) collective-permute-start(bf16[1024,2048]{1,0:T(8,128)(2,1)} %param.6), channel_id=1, source_target_pairs={{0,24},{8,0},{16,8},{24,16},{1,25},{9,1},{17,9},{25,17},{2,26},{10... | collective-permute-start | bytes 12582920 | tf_op jit(solution)/shard_map/ppermute | solution.py:33
  127.8 178.9 %collective-permute-start.2 = (bf16[1024,2048]{1,0:T(8,128)(2,1)}, bf16[1024,2048]{1,0:T(8,128)(2,1)}, u32[]{:S(2)}, u32[]{:S(2)}) collective-permute-start(bf16[1024,2048]{1,0:T(8,128)(2,1)} %collective-permute-done), channel_id=1, source_target_pairs={{0,8},{8,16},{16,24},{24,0},{1,9},{9,17},{17,25},{25,1},{2,10},{10... | collective-permute-start | bytes 12582920 | tf_op jit(solution)/shard_map/ppermute | solution.py:28
  128.8 6.8 copy-start
  795.8 4.0 copy-start.1
  795.8 4.0 copy-start.2
  795.8 368.6 %all-to-all-start.1 = ((bf16[512,32,512]{0,2,1:T(8,128)(2,1)}), bf16[512,32,512]{0,2,1:T(8,128)(2,1)}, u32[]{:S(2)}, u32[]{:S(2)}) async-start(bf16[512,32,512]{0,2,1:T(8,128)(2,1)} %bitcast.19), calls=%async_computation.1 | async-start | bytes 33554432 | tf_op jit(solution)/shard_map/all_to_all | solution.py:45
Sparse Core Ops, SparseCore 0:
  32.2 291.3 all-gather.1
